TPU v7x, 128 devices: a whole 4x4x4 slice. The times are simulated.
128 devices in a mesh: loc: 16 (over x_hi, z, core), inc: 8 (over y, x_lo).
Axes of the slice: x: 4 (x_hi: 2, x_lo: 2; x = x_hi * 2 + x_lo), y: 4, z: 4, core: 2. Of those that a mesh axis runs over, the one named last changes fastest.
Arguments:
- cont_value: float32 [3200, 8192], P('loc', 'inc'), may hold values from -4 to 252, as said below
- flow_util: float32 [3200, 8192], P('loc', 'inc'), may hold values from -6 to 6
- move_cost: float32 [3200, 3200], P('loc'), may hold values from 0 to 6, as said below
- live_mask: int32 [3200], P('loc'), may hold values 0 or 1
- trans_weight: float32 [128, 128], replicated, may hold values from 0.02 to 1
- asset_policy: int32 [128, 64], replicated, may hold values from 0 to 63
- mass: float32 [3200, 8192], P('loc', 'inc'), may hold values from 0.1 to 1
Outputs:
- new_value: float32 [3200, 8192], P('loc', 'inc')
- new_mass: float32 [3200, 8192], P('loc', 'inc')
Inputs may be any that keep to these rules, and one draw needn't show every extreme that they name: cont_value lies within the stated bounds. move_cost is symmetric with a zero diagonal; off the diagonal it lies between 0.5 and 6.
All inputs are finite; a program needn't handle non-finite values. No bound on the sum of `live_mask` on one device may be relied on, other than what follows from the above.
Results may differ from a plain program's by a relative error of at most 0.004.
Values may be sent and summed in bfloat16 or wider, within the bound.
A program may use at most 64 MiB of HBM per device.

v0:
```python
import jax
import jax.numpy as jnp
from jax import lax
from jax.sharding import PartitionSpec as P

E = 128
A = 64


DISCOUNT = 0.96


def shards(cont_value, flow_util, move_cost, live_mask, trans_weight, asset_policy, mass):
    high = lax.Precision.HIGHEST
    local_rows, states = cont_value.shape
    own_incomes = states // A
    first_income = lax.axis_index("inc") * own_incomes
    raised = trans_weight + 16.0 * jnp.eye(E, dtype=jnp.float32)
    trans_prob = raised / jnp.sum(raised, axis=1, keepdims=True)
    onehot = (asset_policy[:, :, None] == jnp.arange(A, dtype=jnp.int32)[None, None, :]).astype(
        jnp.float32
    )
    mine_prob = lax.dynamic_slice_in_dim(trans_prob, first_income, own_incomes, 0)
    mine_hot = lax.dynamic_slice_in_dim(onehot, first_income, own_incomes, 0)
    gathered = lax.all_gather(cont_value, "inc", axis=1, tiled=True)
    expect = jnp.einsum(
        "ef,jfb->jeb", mine_prob, gathered.reshape(local_rows, E, A), precision=high
    )
    chosen = jnp.einsum("jeb,eab->jea", expect, mine_hot, precision=high).reshape(
        local_rows, states
    )
    scores = DISCOUNT * chosen
    live_rows = live_mask[:, None] > 0
    local_max = jnp.max(jnp.where(live_rows, scores, jnp.float32(-1e30)), axis=0)
    column_max = lax.pmax(local_max, "loc")
    dest_weight = jnp.where(
        live_rows, jnp.exp(scores - column_max[None, :]), jnp.float32(0.0)
    ).astype(jnp.bfloat16)
    kernel = jnp.exp(-move_cost).astype(jnp.bfloat16)
    columns = kernel
    totals = jnp.dot(
        columns,
        lax.all_gather(dest_weight, "loc", axis=0, tiled=True),
        preferred_element_type=jnp.float32,
    )
    new_value = flow_util + column_max[None, :] + jnp.log(totals)
    shares = (mass / totals).astype(jnp.bfloat16)
    columns = kernel
    arrived = lax.psum_scatter(
        lax.dot_general(
            columns, shares, (((0,), (0,)), ((), ())), preferred_element_type=jnp.float32
        ).astype(jnp.bfloat16),
        "loc",
        scatter_dimension=0,
        tiled=True,
    ).astype(jnp.float32)
    movers = dest_weight.astype(jnp.float32) * arrived
    shuffled = jnp.einsum(
        "jea,eab->jeb", movers.reshape(local_rows, own_incomes, A), mine_hot, precision=high
    )
    partial_mass = jnp.einsum("ef,jeb->jfb", mine_prob, shuffled, precision=high).reshape(
        local_rows, E * A
    )
    new_mass = lax.psum_scatter(partial_mass, "inc", scatter_dimension=1, tiled=True)
    return (new_value, new_mass)


def solution(mesh):
    return jax.shard_map(
        shards,
        mesh=mesh,
        in_specs=(
            P("loc", "inc"),
            P("loc", "inc"),
            P("loc", None),
            P("loc"),
            P(),
            P(),
            P("loc", "inc"),
        ),
        out_specs=(P("loc", "inc"), P("loc", "inc")),
        check_vma=False,
    )
```

profile of v0, /device:TPU:1, one launch (start us, length us, event | category | flops | bytes accessed | tf_op | source)
XLA Modules:
  0.0 573.1 jit_solution(3270309185936214306)
XLA Ops:
  7.2 0.0 all-gather.3.cloned.1.call-start
  7.2 0.7 all-gather.3.cloned.1.call-update
  7.9 0.0 all-gather.5.cloned.1.call-start
  7.9 0.8 copy.12
  8.8 0.9 fusion.16
  9.8 0.1 dynamic-slice.1
  9.8 0.7 broadcast_compare_fusion
  10.5 136.1 %all-gather.3.cloned.1.call-done = f32[200,8192]{1,0:T(8,128)} async-done(((f32[200,1024]{1,0:T(8,128)}), f32[200,8192]{1,0:T(8,128)}) %all-gather.3.cloned.1.call-update) | async-done | bytes 6553616 | tf_op jit(solution)/shard_map/all_gather | solution.py:25
  146.6 8.6 %copy.13 = f32[200,8192]{0,1:T(8,128)} copy(f32[200,8192]{1,0:T(8,128)} %all-gather.3.cloned.1.call-done) | data formatting | bytes 13107200 | tf_op jit(solution)/shard_map/all_gather | solution.py:25
  155.1 12.4 %fusion = f32[16,200,64]{1,0,2:T(8,128)S(1)} fusion(f32[200,128,64]{0,2,1:T(8,128)} %bitcast.27, f32[128,128]{1,0:T(8,128)S(1)} %get-tuple-element.5, s32[]{:T(128)S(6)} %select_n.13, f32[16]{0:T(128)S(1)} %dynamic-slice.1), kind=kOutput, calls=%fused_computation | convolution fusion | flops 314574848 | bytes 7381508 | tf_op jit(solution)/shard_map/ef,jfb->jeb/dot_general | solution.py:26
  167.5 0.0 copy-start
  167.5 2.4 select_reduce_fusion
  169.9 0.1 reduce_max.12
  169.9 33.7 %pmax.7 = f32[1024]{0:T(1024)S(1)} all-reduce(f32[1024]{0:T(1024)S(1)} %reduce_max.12), channel_id=1, replica_groups=mesh['loc'=16,'inc'=8] {'loc'}, use_global_device_ids=true, to_apply=%region_2.3 | all-reduce | flops 1024 | bytes 8192 | tf_op jit(solution)/shard_map/pmax | solution.py:35
  203.6 1.5 copy.14
  205.1 0.9 select_convert_fusion
  206.0 0.0 all-gather.5.cloned.1.call-update
  206.1 0.0 reduce-scatter.3.cloned.1.call-start
  206.1 66.3 %all-gather.5.cloned.1.call-done = bf16[3200,1024]{1,0:T(8,128)(2,1)} async-done(((bf16[200,1024]{1,0:T(8,128)(2,1)}), bf16[3200,1024]{1,0:T(8,128)(2,1)}) %all-gather.5.cloned.1.call-update) | async-done | bytes 6553616 | tf_op jit(solution)/shard_map/all_gather | solution.py:43
  272.4 0.0 copy-done
  272.4 0.0 copy-start.1
  272.4 5.5 log_add_fusion
  278.0 0.0 copy-done.1
  278.0 4.7 fusion.2
  282.7 0.0 reduce-scatter.3.cloned.1.call-update
  282.7 0.2 reduce-scatter.5.cloned.1.call-start
  283.0 86.9 %reduce-scatter.3.cloned.1.call-done = bf16[200,1024]{1,0:T(8,128)(2,1)} async-done(((bf16[3200,1024]{1,0:T(8,128)(2,1)}), bf16[200,1024]{1,0:T(8,128)(2,1)}) %reduce-scatter.3.cloned.1.call-update) | async-done | bytes 409616 | tf_op jit(solution)/shard_map/reduce_scatter | solution.py:49
  369.9 1.2 convert_multiply_fusion
  371.0 0.3 copy.16
  371.4 0.8 fusion.6
  372.2 0.9 copy.22
  373.1 12.4 %convolution_bitcast_fusion = f32[200,128,64]{1,2,0:T(8,128)} fusion(f32[16,64,200]{1,0,2:T(8,128)S(1)} %copy.22, f32[128,128]{1,0:T(8,128)S(1)} %get-tuple-element.5, s32[]{:T(128)S(6)} %select_n.13, f32[16]{0:T(128)S(1)} %dynamic-slice.1), kind=kOutput, calls=%fused_computation.4 | convolution fusion | flops 314574848 | bytes 8200708 | tf_op jit(solution)/shard_map/ef,jeb->jfb/dot_general | solution.py:61
  385.6 9.1 %copy.17 = f32[200,128,64]{0,2,1:T(8,128)} copy(f32[200,128,64]{1,2,0:T(8,128)} %convolution_bitcast_fusion) | data formatting | bytes 13107200 | tf_op jit(solution)/shard_map/ef,jeb->jfb/transpose | solution.py:61
  394.7 0.0 reduce-scatter.5.cloned.1.call-update
  394.7 169.5 %reduce-scatter.5.cloned.1.call-done = f32[200,1024]{0,1:T(8,128)} async-done(((f32[200,8192]{0,1:T(8,128)}), f32[200,1024]{0,1:T(8,128)}) %reduce-scatter.5.cloned.1.call-update) | async-done | bytes 819216 | tf_op jit(solution)/shard_map/reduce_scatter | solution.py:64
  564.1 2.4 copy.18
  (1 shorter events, 0.0 us)
Async XLA Ops:
  7.2 139.4 %all-gather.3.cloned.1.call-start = ((), (), s32[]{:S(2)}) async-start(), calls=%async_computation.2 | async-start | bytes 7372800 | tf_op jit(solution)/shard_map/all_gather | solution.py:25
  7.9 264.5 %all-gather.5.cloned.1.call-start = ((), (), s32[]{:S(2)}) async-start(), calls=%async_computation.3 | async-start | bytes 6963200 | tf_op jit(solution)/shard_map/all_gather | solution.py:43
  167.5 104.9 %copy-start = (f32[200,3200]{1,0:T(8,128)S(1)}, f32[200,3200]{1,0:T(8,128)}, u32[]{:S(2)}) copy-start(f32[200,3200]{1,0:T(8,128)} %param.9) | copy-start | bytes 7680004
  206.1 163.8 %reduce-scatter.3.cloned.1.call-start = ((), (), s32[]{:S(2)}) async-start(), calls=%async_computation.4 | async-start | bytes 6963200 | tf_op jit(solution)/shard_map/reduce_scatter | solution.py:49
  272.4 5.5 copy-start.1
  282.7 281.4 %reduce-scatter.5.cloned.1.call-start = ((), (), s32[]{:S(2)}) async-start(), calls=%async_computation.5 | async-start | bytes 9437184 | tf_op jit(solution)/shard_map/reduce_scatter | solution.py:64
Sparse Core Ops, SparseCore 0:
  9.6 136.9 all-gather.2
  206.2 66.1 all-gather.4
  282.9 86.9 reduce-scatter.2
  394.8 169.2 reduce-scatter.4
where the time goes:
time: 574 us; the launch traced here: 573 us
  waiting for transfers between devices  459 us (80%)
  matrix products  38.2 us (7%)
  blocking collectives  33.7 us (6%)
  local copies, waits for them, and re-layouts  23.9 us (4%)
  between operations  13.8 us (2%)
    reduce_scatter x1, waiting for transfers between devices, shards(): lax.psum_scatter(partial_mass, 'inc', scatter_dimension=1, tiled=True)  169 us
    all_gather x1, waiting for transfers between devices, shards(): gathered = lax.all_gather(cont_value, 'inc', axis=1, tiled=True)  136 us
    reduce_scatter x1, waiting for transfers between devices, shards(): lax.psum_scatter(lax.dot_general(columns, shares, (((0,), (0,)), ((), ())...  86.9 us
    all_gather x1, waiting for transfers between devices, shards(): lax.all_gather(dest_weight, 'loc', axis=0, tiled=True)  66.3 us
    pmax x1, blocking collectives, shards(): column_max = lax.pmax(local_max, 'loc')  33.7 us
    dot_general x1, matrix products, shards(): jnp.einsum('ef,jeb->jfb', mine_prob, shuffled, precision=high)  12.4 us
    dot_general x1, matrix products, shards(): jnp.einsum('ef,jfb->jeb', mine_prob, gathered.reshape(local_rows, E, A),...  12.4 us
  transfers between devices with their start and end apart: 4, of which 4 were waited for; matrix products, arithmetic and copies ran while one was open for 0% of the time, Pallas kernels for 0%

commit v1 on v0

v1 whole, which is shorter than its diff:
```python
import functools

import jax
import jax.numpy as jnp
from jax import lax
from jax.experimental import pallas as pl
from jax.experimental.pallas import tpu as pltpu
from jax.sharding import PartitionSpec as P

E = 128
A = 64
DISCOUNT = 0.96
NEG = -1e30

MESH = pl.DeviceIdType.MESH
BF = jnp.bfloat16
F32 = jnp.float32

ROWS = 200
PAD = 208
LOC = 16
INC = 8
MINE = ROWS // INC
NC = 2
CW = 1024 // NC
TILES = 8
TPC = TILES // NC


def fold(o, lane_low):
    direct = jnp.where(lane_low, o[0:64], o[192:256])
    cross = jnp.where(lane_low, o[128:192], o[64:128])
    return direct + pltpu.roll(cross, 64, axis=1)


def split3(x):
    a = x.astype(BF)
    r = x - a.astype(F32)
    b = r.astype(BF)
    c = (r - b.astype(F32)).astype(BF)
    return a, b, c


def body(
    cont, flow, mc, live, mass, pfwd, pbwd, gidx, onehot,
    nv_out, nm_out,
    abuf, rbuf, ssend, fbuf, msend, mrecv, kp, bt, dg, ts, tr, town, xs, xr,
    shg, ao, asend, arecv, gbuf, cs, cr, ns, nf,
    lsem, s1, r1, s2, r2, sm, rm, sk, rk, sz, rz, st, rt, sx, rx, sh, rh,
    sa, ra, s3, r3, s4, r4,
):
    li = lax.axis_index("loc")
    ii = lax.axis_index("inc")
    xh = li // 8
    z = lax.rem(li // 2, 4)
    c = lax.rem(li, 2)

    def loc_of(xh_, z_, c_):
        return ((xh_ * 4 + z_) * 2 + c_, ii)

    def inc_of(d):
        return lax.rem(ii + d, INC)

    partner = loc_of(xh, z, 1 - c)
    across = loc_of(1 - xh, z, c)
    pending = []

    def send(src, dst, ssem, rsem, dev):
        cp = pltpu.make_async_remote_copy(
            src_ref=src, dst_ref=dst, send_sem=ssem, recv_sem=rsem,
            device_id=dev, device_id_type=MESH,
        )
        cp.start()
        pending.append(cp)
        return cp

    for k in range(TILES):
        abuf[pl.ds(k, ROWS, stride=8), :] = cont[:, k * 128 : (k + 1) * 128]
    shg[:, :, PAD:256, :] = jnp.zeros((NC, 4, 256 - PAD, CW), BF)

    barrier = pltpu.get_barrier_semaphore()
    for d in range(1, INC):
        pl.semaphore_signal(barrier, inc=1, device_id=(li, inc_of(d)), device_id_type=MESH)
    for d in range(1, LOC):
        pl.semaphore_signal(
            barrier, inc=1, device_id=(lax.rem(li + d, LOC), ii), device_id_type=MESH
        )
    pl.semaphore_wait(barrier, INC - 1 + LOC - 1)

    a2a = []
    for d in range(1, INC):
        peer = inc_of(d)
        a2a.append(send(
            abuf.at[pl.ds(pl.multiple_of(peer * ROWS, 8), ROWS)], rbuf.at[ii],
            s1.at[d], r1.at[d], (li, peer),
        ))
    own1 = pltpu.make_async_copy(
        abuf.at[pl.ds(pl.multiple_of(ii * ROWS, 8), ROWS)], rbuf.at[ii], lsem.at[0]
    )
    own1.start()

    for m in range(LOC):
        first = (m * ROWS) // 128 * 128
        width = 384 if first + 384 <= LOC * ROWS else 256
        shift = m * ROWS - first
        v = mc[:, first : first + width]
        if shift:
            v = pltpu.roll(v, width - shift, axis=1)
        v = jnp.exp(-v[:, :256])
        v = jnp.concatenate([v, jnp.zeros((PAD - ROWS, 256), F32)], axis=0)
        kp[(m // 2) % 4, (m // 8) * 2 + m % 2] = v.astype(BF)
    ksend = []
    for d in (2, 1, 3):
        z2 = lax.rem(z + d, 4)
        ksend.append(send(kp.at[z2], bt.at[z], sk.at[d], rk.at[d], loc_of(xh, z2, c)))
    ownk = pltpu.make_async_copy(kp.at[z], bt.at[z], lsem.at[1])
    ownk.start()

    own1.wait()
    for cp in a2a:
        cp.wait_recv()

    lane_low = lax.broadcasted_iota(jnp.int32, (64, 128), 1) < 64

    @pl.loop(0, 5)
    def _(g):
        base = pl.multiple_of(g * 40, 8)
        blk = rbuf[:, pl.ds(base, 40), :]
        cols = [blk[:, t * 8 : (t + 1) * 8, :].reshape(64, 128) for t in range(5)]
        x = jnp.concatenate(cols, axis=1)
        c1, c2, c3 = split3(x)
        stack = jnp.concatenate([c1, c1, c1, c2, c2, c3], axis=0)
        o = jnp.dot(pfwd[...], stack, preferred_element_type=F32)
        for t in range(5):
            e = fold(o[:, t * 128 : (t + 1) * 128], lane_low)
            s = jnp.take_along_axis(e, gidx[...], axis=1) * DISCOUNT
            ssend[:, pl.ds(pl.multiple_of(base + t * 8, 8), 8), :] = s.reshape(8, 8, 128)

    a2a = []
    for d in range(1, INC):
        peer = inc_of(d)
        a2a.append(send(
            ssend.at[peer], fbuf.at[pl.ds(pl.multiple_of(ii * ROWS, 8), ROWS)],
            s2.at[d], r2.at[d], (li, peer),
        ))
    own2 = pltpu.make_async_copy(
        ssend.at[ii], fbuf.at[pl.ds(pl.multiple_of(ii * ROWS, 8), ROWS)], lsem.at[2]
    )
    own2.start()
    own2.wait()
    for cp in a2a:
        cp.wait_recv()

    alive = live[...] > 0
    for k in range(TILES):
        x = fbuf[pl.ds(k, ROWS, stride=8), :]
        top = jnp.max(jnp.where(alive, x, NEG), axis=0, keepdims=True)
        msend[pl.ds(k, 1), :] = top
    maxes = []
    for d in range(1, LOC):
        maxes.append(send(
            msend, mrecv.at[li], sm.at[d], rm.at[d], (lax.rem(li + d, LOC), ii)
        ))
    ownm = pltpu.make_async_copy(msend, mrecv.at[li], lsem.at[3])
    ownm.start()
    ownm.wait()
    for cp in maxes:
        cp.wait_recv()
    cmax = jnp.max(mrecv[...], axis=0)

    zsend = {}

    def st_d(h):
        for t in range(TPC):
            k = h * TPC + t
            x = fbuf[pl.ds(k, ROWS, stride=8), :]
            w = jnp.where(alive, jnp.exp(x - cmax[k : k + 1, :]), 0.0)
            w = jnp.concatenate([w, jnp.zeros((PAD - ROWS, 128), F32)], axis=0)
            dg[h, z, :, t * 128 : (t + 1) * 128] = w.astype(BF)
        zsend[h] = [
            send(dg.at[h, z], dg.at[h, z], sz.at[h, d], rz.at[h, d],
                 loc_of(xh, lax.rem(z + d, 4), c))
            for d in (2, 1, 3)
        ]

    tsend = {}

    def st_mm1(h):
        if h == 0:
            ownk.wait()
            for cp in ksend:
                cp.wait_recv()
        for cp in zsend[h]:
            cp.wait_recv()
        dall = dg[h].reshape(4 * PAD, CW)
        for mine in (False, True):
            for x2 in range(2):
                p = x2 * 2 + (c if mine else 1 - c)
                lhs = bt[:, p].reshape(4 * PAD, 256)
                t = lax.dot_general(
                    lhs, dall, (((0,), (0,)), ((), ())), preferred_element_type=F32
                )[:PAD]
                if mine:
                    town[h, x2] = t
                else:
                    ts[h, x2] = t.astype(BF)
            if not mine:
                tsend[h] = send(ts.at[h], tr.at[h], st.at[h], rt.at[h], partner)

    xsend = {}

    def st_x(h):
        tsend[h].wait_recv()
        xs[h] = (town[h, 1 - xh] + tr[h, 1 - xh].astype(F32)).astype(BF)
        xsend[h] = send(xs.at[h], xr.at[h], sx.at[h], rx.at[h], across)

    hsend = {}

    def st_share(h):
        xsend[h].wait_recv()
        cols = slice(h * CW, (h + 1) * CW)
        tot = town[h, xh] + tr[h, xh].astype(F32) + xr[h].astype(F32)
        tot = tot[:ROWS]
        lt = jnp.log(tot)
        for t in range(TPC):
            k = h * TPC + t
            wide = slice(k * 128, (k + 1) * 128)
            nv_out[:, wide] = flow[:, wide] + cmax[k : k + 1, :] + lt[:, t * 128 : (t + 1) * 128]
        sv = mass[:, cols] / tot
        sv = jnp.concatenate([sv, jnp.zeros((PAD - ROWS, CW), F32)], axis=0)
        p = xh * 2 + c
        shg[h, p, 0:PAD, :] = sv.astype(BF)
        ref = shg.at[h, p, pl.ds(0, PAD)]
        hsend[h] = [
            send(ref, ref, sh.at[h, 0], rh.at[h, 0], across),
            send(ref, ref, sh.at[h, 1], rh.at[h, 1], partner),
        ]

    def st_fwd(h):
        hsend[h][0].wait_recv()
        ref = shg.at[h, (1 - xh) * 2 + c, pl.ds(0, PAD)]
        hsend[h].append(send(ref, ref, sh.at[h, 2], rh.at[h, 2], partner))

    asends = {}

    def st_mm2(h):
        hsend[h][1].wait_recv()
        hsend[h][2].wait_recv()
        sall = shg[h].reshape(4 * 256, CW)
        asends[h] = []
        for d in (2, 1, 3, 0):
            q = lax.rem(z + d, 4)
            lhs = jnp.concatenate([bt[q, p] for p in range(4)], axis=1)
            a = jnp.dot(lhs, sall, preferred_element_type=F32)
            if d == 0:
                ao[h] = a
            else:
                asend[h, d - 1] = a.astype(BF)
                asends[h].append(send(
                    asend.at[h, d - 1], arecv.at[h, d - 1], sa.at[h, d], ra.at[h, d],
                    loc_of(xh, q, c),
                ))

    def st_move(h):
        for cp in asends[h]:
            cp.wait_recv()
        for t in range(TPC):
            k = h * TPC + t
            lanes = slice(t * 128, (t + 1) * 128)
            arrived = ao[h, :, lanes] + arecv[h, 0, :, lanes].astype(F32)
            arrived = arrived + arecv[h, 1, :, lanes].astype(F32)
            arrived = arrived + arecv[h, 2, :, lanes].astype(F32)
            mv = dg[h, z, :, lanes].astype(F32) * arrived
            hi = mv.astype(BF)
            lo = (mv - hi.astype(F32)).astype(BF)
            sf = jnp.dot(hi, onehot[k], preferred_element_type=F32)
            sf = sf + jnp.dot(lo, onehot[k], preferred_element_type=F32)
            gbuf[pl.ds(k, ROWS, stride=8), :] = sf[:ROWS]

    stages = [st_d, st_mm1, st_x, st_share, st_fwd, st_mm2, st_move]
    for step in range(NC + len(stages) - 1):
        for s in reversed(range(len(stages))):
            if 0 <= step - s < NC:
                stages[s](step - s)

    for i in range(INC):
        blk = gbuf[i * ROWS : (i + 1) * ROWS, :]
        blk = jnp.concatenate([blk, jnp.zeros((PAD - ROWS, 128), F32)], axis=0)
        cs[i] = blk.astype(BF)
    a2a = []
    for d in range(1, INC):
        peer = inc_of(d)
        a2a.append(send(cs.at[peer], cr.at[ii], s3.at[d], r3.at[d], (li, peer)))
    own3 = pltpu.make_async_copy(cs.at[ii], cr.at[ii], lsem.at[4])
    own3.start()
    own3.wait()
    for cp in a2a:
        cp.wait_recv()

    @pl.loop(0, PAD // 16)
    def _(g):
        base = pl.multiple_of(g * 16, 16)
        blk = cr[:, pl.ds(base, 16), :].astype(F32)
        x = jnp.concatenate(
            [blk[:, t * 8 : (t + 1) * 8, :].reshape(64, 128) for t in range(2)], axis=1
        ).astype(BF)
        stack = jnp.concatenate([x, x, x], axis=0)
        o = jnp.dot(pbwd[...], stack, preferred_element_type=F32)
        for t in range(2):
            e = fold(o[:, t * 128 : (t + 1) * 128], lane_low)
            ns[:, pl.ds(pl.multiple_of(base + t * 8, 8), 8), :] = e.reshape(8, 8, 128)

    a2a = []
    for d in range(1, INC):
        peer = inc_of(d)
        a2a.append(send(
            ns.at[peer, pl.ds(0, ROWS)], nf.at[pl.ds(pl.multiple_of(ii * ROWS, 8), ROWS)],
            s4.at[d], r4.at[d], (li, peer),
        ))
    own4 = pltpu.make_async_copy(
        ns.at[ii, pl.ds(0, ROWS)], nf.at[pl.ds(pl.multiple_of(ii * ROWS, 8), ROWS)], lsem.at[5]
    )
    own4.start()
    own4.wait()
    for cp in a2a:
        cp.wait_recv()
    for k in range(TILES):
        nm_out[:, k * 128 : (k + 1) * 128] = nf[pl.ds(k, ROWS, stride=8), :]
    for cp in pending:
        cp.wait_send()


def shards(cont_value, flow_util, move_cost, live_mask, trans_weight, asset_policy, mass):
    raised = trans_weight + 16.0 * jnp.eye(E, dtype=F32)
    prob = raised / jnp.sum(raised, axis=1, keepdims=True)
    four = prob.reshape(64, 2, 64, 2)
    fwd = four.transpose(1, 3, 0, 2).reshape(256, 64)
    bwd = four.transpose(3, 1, 2, 0).reshape(256, 64)
    f1, f2, f3 = split3(fwd)
    b1, b2, b3 = split3(bwd)
    pfwd = jnp.concatenate([f1, f2, f3, f1, f2, f1], axis=1)
    pbwd = jnp.concatenate([b1, b2, b3], axis=1)
    half = (jnp.arange(128, dtype=jnp.int32) // 64) * 64
    gidx = asset_policy.reshape(64, 128) + half[None, :]
    own = lax.dynamic_slice_in_dim(gidx, lax.axis_index("inc") * TILES, TILES, 0)
    onehot = (own[:, :, None] == jnp.arange(128, dtype=jnp.int32)[None, None, :]).astype(BF)
    live = jnp.broadcast_to(live_mask[:, None], (ROWS, 128))

    vm = pl.BlockSpec(memory_space=pltpu.VMEM)
    dma = pltpu.SemaphoreType.DMA
    out = jax.ShapeDtypeStruct((ROWS, 1024), F32)
    return pl.pallas_call(
        body,
        out_shape=(out, out),
        in_specs=[vm] * 9,
        out_specs=(vm, vm),
        scratch_shapes=[
            pltpu.VMEM((8 * ROWS, 128), F32),
            pltpu.VMEM((INC, ROWS, 128), F32),
            pltpu.VMEM((INC, ROWS, 128), F32),
            pltpu.VMEM((8 * ROWS, 128), F32),
            pltpu.VMEM((8, 128), F32),
            pltpu.VMEM((LOC, 8, 128), F32),
            pltpu.VMEM((4, 4, PAD, 256), BF),
            pltpu.VMEM((4, 4, PAD, 256), BF),
            pltpu.VMEM((NC, 4, PAD, CW), BF),
            pltpu.VMEM((NC, 2, PAD, CW), BF),
            pltpu.VMEM((NC, 2, PAD, CW), BF),
            pltpu.VMEM((NC, 2, PAD, CW), F32),
            pltpu.VMEM((NC, PAD, CW), BF),
            pltpu.VMEM((NC, PAD, CW), BF),
            pltpu.VMEM((NC, 4, 256, CW), BF),
            pltpu.VMEM((NC, PAD, CW), F32),
            pltpu.VMEM((NC, 3, PAD, CW), BF),
            pltpu.VMEM((NC, 3, PAD, CW), BF),
            pltpu.VMEM((8 * ROWS, 128), F32),
            pltpu.VMEM((INC, PAD, 128), BF),
            pltpu.VMEM((INC, PAD, 128), BF),
            pltpu.VMEM((INC, PAD, 128), F32),
            pltpu.VMEM((8 * ROWS, 128), F32),
            dma((6,)),
            dma((8,)), dma((8,)), dma((8,)), dma((8,)),
            dma((16,)), dma((16,)), dma((4,)), dma((4,)),
            dma((NC, 4)), dma((NC, 4)), dma((NC,)), dma((NC,)),
            dma((NC,)), dma((NC,)), dma((NC, 3)), dma((NC, 3)),
            dma((NC, 4)), dma((NC, 4)),
            dma((8,)), dma((8,)), dma((8,)), dma((8,)),
        ],
        compiler_params=pltpu.CompilerParams(
            collective_id=0, has_side_effects=True, vmem_limit_bytes=60 * 1024 * 1024
        ),
        name="county_step",
    )(cont_value, flow_util, move_cost, live, mass, pfwd, pbwd, gidx, onehot)


def solution(mesh):
    return jax.shard_map(
        shards,
        mesh=mesh,
        in_specs=(
            P("loc", "inc"),
            P("loc", "inc"),
            P("loc", None),
            P("loc"),
            P(),
            P(),
            P("loc", "inc"),
        ),
        out_specs=(P("loc", "inc"), P("loc", "inc")),
        check_vma=False,
    )
```

time: 574 us -> 149 us (0.26)
  waiting for transfers between devices: 459 us -> 0 us
  Pallas kernels: 0 us -> 127 us
  matrix products: 38.2 us -> 0 us
  blocking collectives: 33.7 us -> 0 us
  between operations: 13.8 us -> 0.72 us
    reduce_scatter x2 -> x0, waiting for transfers between devices: 256 us -> none  [the longest x1 169 us: shards(): lax.psum_scatter(partial_mass, 'inc', scatter_dimension=1, tiled=True)]
    all_gather x2 -> x0, waiting for transfers between devices: 202 us -> none  [the longest x1 136 us: shards(): gathered = lax.all_gather(cont_value, 'inc', axis=1, tiled=True)]
    pallas_call x0 -> x1, Pallas kernels: none -> 127 us  [shards(): pl.pallas_call(body, out_shape=(out, out), in_specs=[vm] * 9, out_specs=(...]
    dot_general x6 -> x0, matrix products: 38.2 us -> none  [the longest x1 12.4 us: shards(): jnp.einsum('ef,jeb->jfb', mine_prob, shuffled, precision=high)]
    pmax x1 -> x0, blocking collectives: 33.7 us -> none  [shards(): column_max = lax.pmax(local_max, 'loc')]
    all_gather x1 -> x0, local copies, waits for them, and re-layouts: 8.55 us -> none  [shards(): gathered = lax.all_gather(cont_value, 'inc', axis=1, tiled=True)]
  transfers between devices with their start and end apart: 4 -> 0, of which waited for: 4 -> 0; matrix products, arithmetic and copies ran while one was open for 0% -> 0% of each run, Pallas kernels for 0% -> 0%
where the time goes in v1:
time: 149 us
  Pallas kernels  127 us (85%)
  local copies, waits for them, and re-layouts  18.2 us (12%)
  other arithmetic  3.63 us (2%)
    pallas_call x1, Pallas kernels, shards(): pl.pallas_call(body, out_shape=(out, out), in_specs=[vm] * 9, out_specs=(...  127 us
    reshape x1, local copies, waits for them, and re-layouts, shards(): four = prob.reshape(64, 2, 64, 2)  5.52 us
    unnamed x9, local copies, waits for them, and re-layouts  4.33 us
    transpose x1, local copies, waits for them, and re-layouts, shards(): bwd = four.transpose(3, 1, 2, 0).reshape(256, 64)  3.68 us

profile of v1, /device:TPU:1, one launch (start us, length us, event | category | flops | bytes accessed | tf_op | source)
XLA Modules:
  0.0 149.2 jit_solution(6290558505416737582)
XLA Ops:
  0.6 0.9 fusion.4
  1.6 0.9 fusion.3
  2.5 5.5 %reshape.33 = f32[64,2,64,2]{3,2,1,0:T(8,128)} reshape(f32[128,128]{1,0:T(8,128)S(1)} %fusion.3) | data formatting | bytes 131072 | tf_op jit(solution)/shard_map/reshape | solution.py:336
  8.0 0.0 copy-start.1
  8.0 3.7 %copy.13 = f32[2,2,64,64]{3,2,1,0:T(8,128)S(1)} copy(f32[2,2,64,64]{0,2,1,3:T(8,128)} %bitcast.28) | data formatting | bytes 131072 | tf_op jit(solution)/shard_map/transpose | solution.py:338
  11.7 0.0 copy-start.2
  11.8 0.8 pad_maximum_fusion.pbwd
  12.5 3.0 %copy.12 = f32[2,2,64,64]{3,2,1,0:T(8,128)S(1)} copy(f32[2,2,64,64]{1,3,0,2:T(8,128)} %bitcast.29) | data formatting | bytes 131072 | tf_op jit(solution)/shard_map/transpose | solution.py:337
  15.6 0.8 concatenate.6.pfwd
  16.4 0.0 copy-done.1
  16.4 0.1 copy.14
  16.5 0.1 reshape.36
  16.6 0.0 copy-start
  16.6 0.9 fusion.onehot
  17.5 0.0 copy-done.2
  17.5 0.7 broadcast_in_dim.2.live
  18.3 0.0 copy-done
  18.3 126.7 %county_step.1 = (f32[200,1024]{1,0:T(8,128)}, f32[200,1024]{1,0:T(8,128)}) custom-call(f32[200,1024]{1,0:T(8,128)} %cont.1, f32[200,1024]{1,0:T(8,128)} %flow.1, f32[200,3200]{1,0:T(8,128)} %mc.1, s32[200,128]{1,0:T(8,128)} %broadcast_in_dim.2.live, f32[200,1024]{1,0:T(8,128)} %mass.1, bf16[256,384]{1,0:T(8,128)(2,1)} %concatenate.6.pfwd, ...), custom_call_target="tpu_custom_call" | custom-call | tf_op jit(solution)/shard_map/county_step/pallas_call | solution.py:352
  144.9 2.1 %copy.17 = f32[200,1024]{1,0:T(8,128)} copy(f32[200,1024]{1,0:T(8,128)} %get-tuple-element.8) | data formatting | bytes 1638400
  147.1 2.1 %copy.18 = f32[200,1024]{1,0:T(8,128)} copy(f32[200,1024]{1,0:T(8,128)} %get-tuple-element.9) | data formatting | bytes 1638400
  (7 shorter events, 0.1 us)
Async XLA Ops:
  8.0 8.4 %copy-start.1 = (s32[128,64]{0,1:T(8,128)S(1)}, s32[128,64]{0,1:T(8,128)}, u32[]{:S(2)}) copy-start(s32[128,64]{0,1:T(8,128)} %param.12) | copy-start | bytes 98308
  11.7 5.8 %copy-start.2 = (s32[200]{0:T(256)S(1)}, s32[200]{0:T(256)}, u32[]{:S(2)}) copy-start(s32[200]{0:T(256)} %param.10) | copy-start | bytes 2404
  16.6 1.7 %copy-start = (s32[64,128]{1,0:T(8,128)}, s32[64,128]{1,0:T(8,128)S(1)}, u32[]{:S(2)}) copy-start(s32[64,128]{1,0:T(8,128)S(1)} %broadcast_add_fusion.gidx) | copy-start | bytes 98308

commit v2 on v0

v2 whole, which is shorter than its diff:
```python
import jax
import jax.numpy as jnp
from jax import lax
from jax.experimental import pallas as pl
from jax.experimental.pallas import tpu as pltpu
from jax.sharding import PartitionSpec as P

E = 128
A = 64
DISCOUNT = 0.96
DEAD = 1e30

MESH = pl.DeviceIdType.MESH
BF = jnp.bfloat16
F32 = jnp.float32

ROWS = 200
INC = 8
MINE = ROWS // INC
PLANE = 16
L = 3200
NC = 2
TPC = 4 // NC
CW = TPC * 128
PIECE = TPC * MINE


def fold(o, lane_low):
    direct = jnp.where(lane_low, o[0:64], o[192:256])
    cross = jnp.where(lane_low, o[128:192], o[64:128])
    return direct + pltpu.roll(cross, 64, axis=1)


def split3(x):
    a = x.astype(BF)
    r = x - a.astype(F32)
    b = r.astype(BF)
    c = (r - b.astype(F32)).astype(BF)
    return a, b, c


def body(
    cont_h, mc_h, mass_h, live, tw, pol,
    v_out, nm_out,
    cont, mc, mass,
    abuf, rbuf, sb, ssend, msd, mrv, mds, mdr, fb, fc, kp, dall, shall, mz, msnd,
    tots, vsend, sfr, csf, cs, cr, xf, ns,
    pscr, ptscr, pfwd, pbwd, onehot,
    lsem, s1, r1, s2, r2, sm, rm, sd, rd, sk, rk, sg, rg, sv, rv, s3, r3, s4, r4,
):
    li = lax.axis_index("loc")
    ii = lax.axis_index("inc")
    xh = li // 8
    z = lax.rem(li // 2, 4)
    c = lax.rem(li, 2)
    g = ii * 2 + xh
    slot = xh * 8 + ii
    blk = z * 2 + c

    def dev(xh_, z_, c_, ii_):
        return ((xh_ * 4 + z_) * 2 + c_, ii_)

    up = lax.rem(z + 1, 4)
    down = lax.rem(z + 3, 4)
    far = lax.rem(z + 2, 4)
    partner = dev(xh, z, 1 - c, ii)
    across = dev(1 - xh, z, c, ii)
    pending = []

    def send(src, dst, ssem, rsem, to):
        cp = pltpu.make_async_remote_copy(
            src_ref=src, dst_ref=dst, send_sem=ssem, recv_sem=rsem,
            device_id=to, device_id_type=MESH,
        )
        cp.start()
        pending.append(cp)
        return cp

    def local(src, dst, k):
        cp = pltpu.make_async_copy(src, dst, lsem.at[k])
        cp.start()
        return cp

    in1 = local(cont_h, cont, 0)
    in2 = local(mc_h, mc, 1)
    in3 = local(mass_h, mass, 2)

    barrier = pltpu.get_barrier_semaphore()
    plane = []
    for d in range(1, PLANE):
        g2 = lax.rem(g + d, PLANE)
        plane.append((g2, dev(lax.rem(g2, 2), z, c, g2 // 2), lax.rem(g2, 2) * 8 + g2 // 2))
    column = []
    for d in range(1, 8):
        b2 = lax.rem(blk + d, 8)
        column.append(dev(xh, b2 // 2, lax.rem(b2, 2), ii))
    for _, to, _ in plane:
        pl.semaphore_signal(barrier, inc=1, device_id=to, device_id_type=MESH)
    for to in column:
        pl.semaphore_signal(barrier, inc=1, device_id=to, device_id_type=MESH)

    in1.wait()
    for k in range(8):
        abuf[pl.ds(k, ROWS, stride=8), :] = cont[:, k * 128 : (k + 1) * 128]
    pl.semaphore_wait(barrier, PLANE - 1 + 7)

    a2a = []
    for d in range(1, INC):
        peer = lax.rem(ii + d, INC)
        a2a.append(send(
            abuf.at[pl.ds(pl.multiple_of(peer * ROWS, 8), ROWS)], rbuf.at[ii],
            s1.at[d], r1.at[d], (li, peer),
        ))
    own1 = local(abuf.at[pl.ds(pl.multiple_of(ii * ROWS, 8), ROWS)], rbuf.at[ii], 3)

    in2.wait()
    for x2 in range(2):
        for b in range(8):
            src = (x2 * 8 + b) * ROWS
            dst = (b * 2 + x2) * ROWS
            kp[xh, :, dst : dst + ROWS] = jnp.exp(-mc[:, src : src + ROWS]).astype(BF)
    ksend = send(kp.at[xh], kp.at[xh], sk.at[0], rk.at[0], across)

    in3.wait()
    mz[xh] = mass[:, pl.ds(pl.multiple_of(xh * 512, 512), 512)].astype(BF)
    msnd[...] = mass[:, pl.ds(pl.multiple_of((1 - xh) * 512, 512), 512)].astype(BF)
    msend = send(msnd, mz.at[xh], sk.at[1], rk.at[1], across)

    row = lax.broadcasted_iota(jnp.int32, (128, 128), 0)
    col = lax.broadcasted_iota(jnp.int32, (128, 128), 1)
    raised = tw[...] + jnp.where(row == col, 16.0, 0.0)
    prob = raised / jnp.sum(raised, axis=1, keepdims=True)
    pscr[...] = prob
    ptscr[...] = prob.T

    def pick(parity, high):
        want = col - 64 if high else col
        keep = (want >= 0) & (want < 64) & (row == 2 * want + parity)
        return jnp.where(keep, 1.0, 0.0).astype(BF)

    for scr, out, pairs in (
        (pscr, pfwd, ((0, 1), (2, 0), (1, 0))),
        (ptscr, pbwd, ((0, 1), (2, None))),
    ):
        for po in range(2):
            parts = split3(scr[pl.ds(po, 64, stride=2), :])
            for pi in range(2):
                low, high = pick(pi, False), pick(pi, True)
                for n, (a, b) in enumerate(pairs):
                    q = jnp.dot(parts[a], low, preferred_element_type=F32)
                    if b is not None:
                        q = q + jnp.dot(parts[b], high, preferred_element_type=F32)
                    r0 = (po * 2 + pi) * 64
                    out[r0 : r0 + 64, n * 128 : (n + 1) * 128] = q.astype(BF)

    lane64 = lax.broadcasted_iota(jnp.int32, (64, 128), 1)
    lane_low = lane64 < 64
    gidx = pol[...] + jnp.where(lane_low, 0, 64)
    gown = pol[pl.ds(g * 4, 4), :] + jnp.where(col[0:4] < 64, 0, 64)
    for t in range(4):
        wide = jnp.broadcast_to(gown[t : t + 1].astype(F32), (128, 128)).T
        onehot[t] = jnp.where(wide == col.astype(F32), 1.0, 0.0).astype(BF)

    own1.wait()
    for cp in a2a:
        cp.wait_recv()

    def mix(i, top):
        base = pl.multiple_of(i * 40, 8)
        piece = rbuf[:, pl.ds(base, 40), :]
        cols = [piece[:, t * 8 : (t + 1) * 8, :].reshape(64, 128) for t in range(5)]
        c1, c2, c3 = split3(jnp.concatenate(cols, axis=1))
        stack = jnp.concatenate([c1, c1, c1, c2, c2, c3], axis=0)
        o = jnp.dot(pfwd[...], stack, preferred_element_type=F32)
        for t in range(5):
            e = fold(o[:, t * 128 : (t + 1) * 128], lane_low)
            s = jnp.take_along_axis(e, gidx, axis=1) * DISCOUNT
            alive = live[ii * MINE + i * 5 + t].astype(F32)
            s = s + (alive - 1.0) * DEAD
            top = jnp.maximum(top, s)
            sb[pl.ds(pl.multiple_of((i * 5 + t) * 64, 64), 64), :] = s
        return top

    top = lax.fori_loop(0, 5, mix, jnp.full((64, 128), -2 * DEAD, F32))
    for k in range(PLANE):
        msd[k] = top[k * 4 : (k + 1) * 4]
    tops = [
        send(msd.at[g2], mrv.at[slot], sm.at[d + 1], rm.at[d + 1], to)
        for d, (g2, to, _) in enumerate(plane)
    ]
    ownm = local(msd.at[g], mrv.at[slot], 4)
    scat = {}
    owns = {}
    for h in range(NC):
        for k in range(PLANE):
            for t in range(TPC):
                tile = k * 4 + h * TPC + t
                ssend[h, k, t * MINE : (t + 1) * MINE, :] = sb[pl.ds(tile, MINE, stride=64), :]
        scat[h] = [
            send(ssend.at[h, g2], fb.at[h, slot], s2.at[h, d + 1], r2.at[h, d + 1], to)
            for d, (g2, to, _) in enumerate(plane)
        ]
        owns[h] = local(ssend.at[h, g], fb.at[h, slot], 5 + h)

    ownm.wait()
    for cp in tops:
        cp.wait_recv()
    mds[...] = jnp.max(mrv[...], axis=0)
    maxes = [
        send(mds, mdr.at[blk], sd.at[d + 1], rd.at[d + 1], to)
        for d, to in enumerate(column)
    ]
    mdr[blk] = mds[...]
    for cp in maxes:
        cp.wait_recv()
    cmax = jnp.max(mdr[...], axis=0)

    my_rows = pl.ds(pl.multiple_of(blk * 400, 16), 400)

    def rows_of(z_, c_):
        return pl.ds(pl.multiple_of((z_ * 2 + c_) * 400, 16), 400)

    got = {}

    def gather0(n, buf, h):
        ref = buf.at[h, my_rows]
        got[n, h] = [
            send(ref, ref, sg.at[n, h, 0], rg.at[n, h, 0], dev(xh, up, c, ii)),
            send(ref, ref, sg.at[n, h, 1], rg.at[n, h, 1], dev(xh, down, c, ii)),
            send(ref, ref, sg.at[n, h, 2], rg.at[n, h, 2], partner),
        ]

    def gather1(n, buf, h):
        w = got[n, h]
        for k, (src, to) in enumerate(((down, up), (up, down))):
            w[k].wait_recv()
            half = buf.at[h, rows_of(src, c), pl.ds(k * (CW // 2), CW // 2)]
            w.append(send(half, half, sg.at[n, h, 3 + k], rg.at[n, h, 3 + k], dev(xh, to, c, ii)))
            ref = buf.at[h, rows_of(src, c)]
            w.append(send(ref, ref, sg.at[n, h, 5 + k], rg.at[n, h, 5 + k], partner))

    def gather2(n, buf, h):
        w = got[n, h]
        for k, cp in enumerate((w[3], w[5])):
            cp.wait_recv()
            half = buf.at[h, rows_of(far, c), pl.ds(k * (CW // 2), CW // 2)]
            w.append(send(half, half, sg.at[n, h, 7 + k], rg.at[n, h, 7 + k], partner))

    def gather3(n, buf, h):
        w = got[n, h]
        for cp in (w[2], w[4], w[6], w[7], w[8]):
            cp.wait_recv()

    def st_d(h):
        owns[h].wait()
        for cp in scat[h]:
            cp.wait_recv()
        for t in range(TPC):
            for k in range(PLANE):
                fc[k * MINE : (k + 1) * MINE, t * 128 : (t + 1) * 128] = fb[
                    h, k, t * MINE : (t + 1) * MINE, :
                ]
        for t in range(TPC):
            k = h * TPC + t
            lanes = slice(t * 128, (t + 1) * 128)
            dall[h, my_rows, lanes] = jnp.exp(fc[:, lanes] - cmax[k : k + 1, :]).astype(BF)
        gather0(0, dall, h)

    def st_share(h):
        gather3(0, dall, h)
        if h == 0:
            ksend.wait_recv()
            msend.wait_recv()
        for x2 in range(2):
            tots[x2] = jnp.dot(kp[x2], dall[h], preferred_element_type=F32)
        sh = []
        for x2 in range(2):
            sh.append(mz[x2, :, h * CW : (h + 1) * CW].astype(F32) / tots[x2])
        shall[h, my_rows, :] = jnp.concatenate(sh, axis=0).astype(BF)
        gather0(1, shall, h)
        cm = jnp.concatenate([cmax[h * TPC + t : h * TPC + t + 1, :] for t in range(TPC)], axis=1)
        cols = pl.ds(pl.multiple_of(xh * 512 + h * CW, 128), CW)
        v_out[:, cols] = cm + jnp.log(tots[xh])
        vsend[h] = cm + jnp.log(tots[1 - xh])
        vs.append(send(vsend.at[h], v_out.at[:, cols], sv.at[h], rv.at[h], across))

    vs = []
    back = {}
    ownb = {}

    def st_move(h):
        gather3(1, shall, h)
        for x2 in range(2):
            tots[x2] = jnp.dot(kp[x2], shall[h], preferred_element_type=F32)
        arrived = jnp.concatenate([tots[0], tots[1]], axis=0)
        for t in range(TPC):
            lanes = slice(t * 128, (t + 1) * 128)
            mv = dall[h, my_rows, lanes].astype(F32) * arrived[:, lanes]
            hi = mv.astype(BF)
            lo = (mv - hi.astype(F32)).astype(BF)
            oh = onehot[h * TPC + t]
            sfr[...] = jnp.dot(hi, oh, preferred_element_type=F32) + jnp.dot(
                lo, oh, preferred_element_type=F32
            )
            for k in range(PLANE):
                csf[k, t * MINE : (t + 1) * MINE, :] = sfr[k * MINE : (k + 1) * MINE, :]
        for k in range(PLANE):
            cs[h, k] = csf[k].astype(BF)
        back[h] = [
            send(cs.at[h, s2_], cr.at[h, g], s3.at[h, d + 1], r3.at[h, d + 1], to)
            for d, (_, to, s2_) in enumerate(plane)
        ]
        ownb[h] = local(cs.at[h, slot], cr.at[h, g], 5 + NC + h)

    stages = [
        st_d,
        lambda h: gather1(0, dall, h),
        lambda h: gather2(0, dall, h),
        st_share,
        lambda h: gather1(1, shall, h),
        lambda h: gather2(1, shall, h),
        st_move,
    ]
    for step in range(NC + len(stages) - 1):
        for s in reversed(range(len(stages))):
            if 0 <= step - s < NC:
                stages[s](step - s)

    for h in range(NC):
        ownb[h].wait()
        for cp in back[h]:
            cp.wait_recv()
        for k in range(PLANE):
            first = k * 4 * MINE + h * PIECE
            xf[first : first + PIECE, :] = cr[h, k].astype(F32)

    @pl.loop(0, 5)
    def _(i):
        x = jnp.concatenate(
            [xf[pl.ds(i * 5 + t, 64, stride=MINE), :] for t in range(5)], axis=1
        ).astype(BF)
        stack = jnp.concatenate([x, x, x, x], axis=0)
        o = jnp.dot(pbwd[...], stack, preferred_element_type=F32)
        for t in range(5):
            e = fold(o[:, t * 128 : (t + 1) * 128], lane_low)
            ns[:, pl.ds(pl.multiple_of(i * 40 + t * 8, 8), 8), :] = e.reshape(8, 8, 128)

    mine = pl.ds(pl.multiple_of(ii * ROWS, 8), ROWS)
    a2a = []
    for d in range(1, INC):
        peer = lax.rem(ii + d, INC)
        a2a.append(send(ns.at[peer], nm_out.at[mine], s4.at[d], r4.at[d], (li, peer)))
    own4 = local(ns.at[ii], nm_out.at[mine], 5 + 2 * NC)
    own4.wait()
    for cp in a2a:
        cp.wait_recv()
    for cp in vs:
        cp.wait_recv()
    for cp in pending:
        cp.wait_send()


def shards(cont_value, flow_util, move_cost, live_mask, trans_weight, asset_policy, mass):
    vm = pl.BlockSpec(memory_space=pltpu.VMEM)
    any_ = pl.BlockSpec(memory_space=pl.ANY)
    dma = pltpu.SemaphoreType.DMA
    v, nm = pl.pallas_call(
        body,
        out_shape=(
            jax.ShapeDtypeStruct((ROWS, 1024), F32),
            jax.ShapeDtypeStruct((8 * ROWS, 128), F32),
        ),
        in_specs=[any_, any_, any_, pl.BlockSpec(memory_space=pltpu.SMEM), vm, vm],
        out_specs=(vm, vm),
        scratch_shapes=[
            pltpu.VMEM((ROWS, 1024), F32),
            pltpu.VMEM((ROWS, L), F32),
            pltpu.VMEM((ROWS, 1024), F32),
            pltpu.VMEM((8 * ROWS, 128), F32),
            pltpu.VMEM((INC, ROWS, 128), F32),
            pltpu.VMEM((MINE * 64, 128), F32),
            pltpu.VMEM((NC, PLANE, PIECE, 128), F32),
            pltpu.VMEM((PLANE, 4, 128), F32),
            pltpu.VMEM((PLANE, 4, 128), F32),
            pltpu.VMEM((4, 128), F32),
            pltpu.VMEM((8, 4, 128), F32),
            pltpu.VMEM((NC, PLANE, PIECE, 128), F32),
            pltpu.VMEM((2 * ROWS, CW), F32),
            pltpu.VMEM((2, ROWS, L), BF),
            pltpu.VMEM((NC, L, CW), BF),
            pltpu.VMEM((NC, L, CW), BF),
            pltpu.VMEM((2, ROWS, 512), BF),
            pltpu.VMEM((ROWS, 512), BF),
            pltpu.VMEM((2, ROWS, CW), F32),
            pltpu.VMEM((NC, ROWS, CW), F32),
            pltpu.VMEM((2 * ROWS, 128), F32),
            pltpu.VMEM((PLANE, PIECE, 128), F32),
            pltpu.VMEM((NC, PLANE, PIECE, 128), BF),
            pltpu.VMEM((NC, PLANE, PIECE, 128), BF),
            pltpu.VMEM((MINE * 64, 128), F32),
            pltpu.VMEM((INC, ROWS, 128), F32),
            pltpu.VMEM((128, 128), F32),
            pltpu.VMEM((128, 128), F32),
            pltpu.VMEM((256, 384), BF),
            pltpu.VMEM((256, 256), BF),
            pltpu.VMEM((4, 128, 128), BF),
            dma((6 + 2 * NC,)),
            dma((8,)), dma((8,)), dma((NC, 16)), dma((NC, 16)),
            dma((16,)), dma((16,)), dma((8,)), dma((8,)),
            dma((2,)), dma((2,)), dma((2, NC, 9)), dma((2, NC, 9)),
            dma((NC,)), dma((NC,)), dma((NC, 16)), dma((NC, 16)),
            dma((8,)), dma((8,)),
        ],
        compiler_params=pltpu.CompilerParams(
            collective_id=0, has_side_effects=True, vmem_limit_bytes=60 * 1024 * 1024
        ),
        name="county_step",
    )(cont_value, move_cost, mass, live_mask, trans_weight, asset_policy.reshape(64, 128))
    return flow_util + v, nm.reshape(ROWS, 1024)


def solution(mesh):
    return jax.shard_map(
        shards,
        mesh=mesh,
        in_specs=(
            P("loc", "inc"),
            P("loc", "inc"),
            P("loc", None),
            P("loc"),
            P(),
            P(),
            P("loc", "inc"),
        ),
        out_specs=(P("loc", "inc"), P("loc", "inc")),
        check_vma=False,
    )
```

time: 574 us -> 122 us (0.21)
  waiting for transfers between devices: 459 us -> 0 us
  Pallas kernels: 0 us -> 116 us
  matrix products: 38.2 us -> 0 us
  blocking collectives: 33.7 us -> 0 us
  local copies, waits for them, and re-layouts: 23.9 us -> 2.64 us
  between operations: 13.8 us -> 0.67 us
    reduce_scatter x2 -> x0, waiting for transfers between devices: 256 us -> none  [the longest x1 169 us: shards(): lax.psum_scatter(partial_mass, 'inc', scatter_dimension=1, tiled=True)]
    all_gather x2 -> x0, waiting for transfers between devices: 202 us -> none  [the longest x1 136 us: shards(): gathered = lax.all_gather(cont_value, 'inc', axis=1, tiled=True)]
    pallas_call x0 -> x1, Pallas kernels: none -> 116 us  [shards(): pl.pallas_call(body, out_shape=(jax.ShapeDtypeStruct((ROWS, 1024), F32),...]
    dot_general x6 -> x0, matrix products: 38.2 us -> none  [the longest x1 12.4 us: shards(): jnp.einsum('ef,jeb->jfb', mine_prob, shuffled, precision=high)]
    pmax x1 -> x0, blocking collectives: 33.7 us -> none  [shards(): column_max = lax.pmax(local_max, 'loc')]
    transpose x1 -> x0, local copies, waits for them, and re-layouts: 9.09 us -> none  [shards(): jnp.einsum('ef,jeb->jfb', mine_prob, shuffled, precision=high)]
    all_gather x1 -> x0, local copies, waits for them, and re-layouts: 8.55 us -> none  [shards(): gathered = lax.all_gather(cont_value, 'inc', axis=1, tiled=True)]
  transfers between devices with their start and end apart: 4 -> 0, of which waited for: 4 -> 0; matrix products, arithmetic and copies ran while one was open for 0% -> 0% of each run, Pallas kernels for 0% -> 0%
where the time goes in v2:
time: 122 us
  Pallas kernels  116 us (95%)
  local copies, waits for them, and re-layouts  2.64 us (2%)
  other arithmetic  2.21 us (2%)
    pallas_call x1, Pallas kernels, shards(): pl.pallas_call(body, out_shape=(jax.ShapeDtypeStruct((ROWS, 1024), F32),...  116 us

profile of v2, /device:TPU:1, one launch (start us, length us, event | category | flops | bytes accessed | tf_op | source)
XLA Modules:
  0.0 122.0 jit_solution(16593620720199951441)
XLA Ops:
  0.6 0.0 copy-start
  0.6 0.9 copy.10
  1.6 0.7 reshape.10.pol
  2.3 116.5 %county_step.1 = (f32[200,1024]{1,0:T(8,128)}, f32[1600,128]{1,0:T(8,128)}) custom-call(f32[200,1024]{1,0:T(8,128)} %cont_h.1, f32[200,3200]{1,0:T(8,128)} %mc_h.1, f32[200,1024]{1,0:T(8,128)} %mass_h.1, s32[200]{0:T(256)} %live.1, f32[128,128]{1,0:T(8,128)} %tw.1, s32[64,128]{1,0:T(8,128)} %reshape.10.pol), custom_call_target="tpu_custom_call" | custom-call | tf_op jit(solution)/shard_map/county_step/pallas_call | solution.py:367
  118.7 0.0 copy-start.1
  118.7 0.0 copy-done
  118.7 2.2 %add.3 = f32[200,1024]{1,0:T(8,128)} add(f32[200,1024]{1,0:T(8,128)S(1)} %copy-done, f32[200,1024]{1,0:T(8,128)} %get-tuple-element.4) | non-fusion elementwise | flops 204800 | bytes 2457600 | tf_op jit(solution)/shard_map/add | solution.py:419
  120.9 0.0 copy-done.1
  120.9 1.0 reshape.11
Async XLA Ops:
  0.6 118.1 %copy-start = (f32[200,1024]{1,0:T(8,128)S(1)}, f32[200,1024]{1,0:T(8,128)}, u32[]{:S(2)}) copy-start(f32[200,1024]{1,0:T(8,128)} %param.8) | copy-start | bytes 2457604
  118.7 2.2 %copy-start.1 = (f32[1600,128]{1,0:T(8,128)S(1)}, f32[1600,128]{1,0:T(8,128)}, u32[]{:S(2)}) copy-start(f32[1600,128]{1,0:T(8,128)} %get-tuple-element.5) | copy-start | bytes 2457604

commit v3 on v2

--- a/solution.py
+++ b/solution.py
@@ -43,9 +43,9 @@
     cont_h, mc_h, mass_h, live, tw, pol,
     v_out, nm_out,
     cont, mc, mass,
-    abuf, rbuf, sb, ssend, msd, mrv, mds, mdr, fb, fc, kp, dall, shall, mz, msnd,
-    tots, vsend, sfr, csf, cs, cr, xf, ns,
-    pscr, ptscr, pfwd, pbwd, onehot,
+    ko, kt, kr, abuf, rbuf, sb, ssend, msd, mrv, mds, mdr, fb, fc, kp, dall, shall, mz, msnd,
+    tots, vown, vsend, sfr, csf, cs, cr, xf, ns,
+    gsc, pscr, ptscr, pfwd, pbwd, onehot,
     lsem, s1, r1, s2, r2, sm, rm, sd, rd, sk, rk, sg, rg, sv, rv, s3, r3, s4, r4,
 ):
     li = lax.axis_index("loc")
@@ -102,7 +102,18 @@
     in1.wait()
     for k in range(8):
         abuf[pl.ds(k, ROWS, stride=8), :] = cont[:, k * 128 : (k + 1) * 128]
+    in2.wait()
+    for x2 in range(2):
+
+        @pl.when(xh == x2)
+        def _():
+            for b in range(8):
+                src = (x2 * 8 + b) * ROWS
+                ko[b] = jnp.exp(-mc[:, src : src + ROWS]).astype(BF)
+
     pl.semaphore_wait(barrier, PLANE - 1 + 7)
+    beside = dev(1 - xh, z, c, ii + 1 - 2 * lax.rem(ii, 2))
+    ksend = [send(ko, kr.at[xh], sk.at[0], rk.at[0], beside)]
 
     a2a = []
     for d in range(1, INC):
@@ -113,18 +124,22 @@
         ))
     own1 = local(abuf.at[pl.ds(pl.multiple_of(ii * ROWS, 8), ROWS)], rbuf.at[ii], 3)
 
-    in2.wait()
     for x2 in range(2):
         for b in range(8):
             src = (x2 * 8 + b) * ROWS
             dst = (b * 2 + x2) * ROWS
             kp[xh, :, dst : dst + ROWS] = jnp.exp(-mc[:, src : src + ROWS]).astype(BF)
-    ksend = send(kp.at[xh], kp.at[xh], sk.at[0], rk.at[0], across)
-
-    in3.wait()
-    mz[xh] = mass[:, pl.ds(pl.multiple_of(xh * 512, 512), 512)].astype(BF)
-    msnd[...] = mass[:, pl.ds(pl.multiple_of((1 - xh) * 512, 512), 512)].astype(BF)
-    msend = send(msnd, mz.at[xh], sk.at[1], rk.at[1], across)
+
+        @pl.when(xh != x2)
+        def _():
+            for b in range(8):
+                src = (x2 * 8 + b) * ROWS
+                kt[b] = jnp.exp(-mc[:, src : src + ROWS]).T.astype(BF)
+
+    for d, to in enumerate(column):
+        b2 = lax.rem(blk + d + 1, 8)
+        ksend.append(send(kt.at[b2], kr.at[xh, blk], sk.at[2 + d], rk.at[2 + d], to))
+    ownk = local(kt.at[blk], kr.at[xh, blk], 6 + 2 * NC)
 
     row = lax.broadcasted_iota(jnp.int32, (128, 128), 0)
     col = lax.broadcasted_iota(jnp.int32, (128, 128), 1)
@@ -155,8 +170,11 @@
 
     lane64 = lax.broadcasted_iota(jnp.int32, (64, 128), 1)
     lane_low = lane64 < 64
-    gidx = pol[...] + jnp.where(lane_low, 0, 64)
-    gown = pol[pl.ds(g * 4, 4), :] + jnp.where(col[0:4] < 64, 0, 64)
+    gsc[...] = jnp.concatenate(
+        [pol[pl.ds(0, 64, stride=2), :], pol[pl.ds(1, 64, stride=2), :] + 64], axis=1
+    )
+    gidx = gsc[...]
+    gown = gsc[pl.ds(g * 4, 4), :]
     for t in range(4):
         wide = jnp.broadcast_to(gown[t : t + 1].astype(F32), (128, 128)).T
         onehot[t] = jnp.where(wide == col.astype(F32), 1.0, 0.0).astype(BF)
@@ -202,6 +220,11 @@
         ]
         owns[h] = local(ssend.at[h, g], fb.at[h, slot], 5 + h)
 
+    in3.wait()
+    mz[xh] = mass[:, pl.ds(pl.multiple_of(xh * 512, 512), 512)].astype(BF)
+    msnd[...] = mass[:, pl.ds(pl.multiple_of((1 - xh) * 512, 512), 512)].astype(BF)
+    msend = send(msnd, mz.at[xh], sk.at[1], rk.at[1], across)
+
     ownm.wait()
     for cp in tops:
         cp.wait_recv()
@@ -214,6 +237,14 @@
     for cp in maxes:
         cp.wait_recv()
     cmax = jnp.max(mdr[...], axis=0)
+
+    ownk.wait()
+    for cp in ksend:
+        cp.wait_recv()
+    for x2 in range(2):
+        for b in range(8):
+            dst = (b * 2 + x2) * ROWS
+            kp[1 - xh, :, dst : dst + ROWS] = kr[x2, b]
 
     my_rows = pl.ds(pl.multiple_of(blk * 400, 16), 400)
 
@@ -269,7 +300,6 @@
     def st_share(h):
         gather3(0, dall, h)
         if h == 0:
-            ksend.wait_recv()
             msend.wait_recv()
         for x2 in range(2):
             tots[x2] = jnp.dot(kp[x2], dall[h], preferred_element_type=F32)
@@ -280,11 +310,13 @@
         gather0(1, shall, h)
         cm = jnp.concatenate([cmax[h * TPC + t : h * TPC + t + 1, :] for t in range(TPC)], axis=1)
         cols = pl.ds(pl.multiple_of(xh * 512 + h * CW, 128), CW)
-        v_out[:, cols] = cm + jnp.log(tots[xh])
+        vown[h] = cm + jnp.log(tots[xh])
+        ownv.append(local(vown.at[h], v_out.at[:, cols], 7 + 2 * NC + h))
         vsend[h] = cm + jnp.log(tots[1 - xh])
         vs.append(send(vsend.at[h], v_out.at[:, cols], sv.at[h], rv.at[h], across))
 
     vs = []
+    ownv = []
     back = {}
     ownb = {}
 
@@ -354,6 +386,8 @@
     own4.wait()
     for cp in a2a:
         cp.wait_recv()
+    for cp in ownv:
+        cp.wait()
     for cp in vs:
         cp.wait_recv()
     for cp in pending:
@@ -371,11 +405,14 @@
             jax.ShapeDtypeStruct((8 * ROWS, 128), F32),
         ),
         in_specs=[any_, any_, any_, pl.BlockSpec(memory_space=pltpu.SMEM), vm, vm],
-        out_specs=(vm, vm),
+        out_specs=(any_, any_),
         scratch_shapes=[
             pltpu.VMEM((ROWS, 1024), F32),
             pltpu.VMEM((ROWS, L), F32),
             pltpu.VMEM((ROWS, 1024), F32),
+            pltpu.VMEM((8, ROWS, ROWS), BF),
+            pltpu.VMEM((8, ROWS, ROWS), BF),
+            pltpu.VMEM((2, 8, ROWS, ROWS), BF),
             pltpu.VMEM((8 * ROWS, 128), F32),
             pltpu.VMEM((INC, ROWS, 128), F32),
             pltpu.VMEM((MINE * 64, 128), F32),
@@ -393,21 +430,23 @@
             pltpu.VMEM((ROWS, 512), BF),
             pltpu.VMEM((2, ROWS, CW), F32),
             pltpu.VMEM((NC, ROWS, CW), F32),
+            pltpu.VMEM((NC, ROWS, CW), F32),
             pltpu.VMEM((2 * ROWS, 128), F32),
             pltpu.VMEM((PLANE, PIECE, 128), F32),
             pltpu.VMEM((NC, PLANE, PIECE, 128), BF),
             pltpu.VMEM((NC, PLANE, PIECE, 128), BF),
             pltpu.VMEM((MINE * 64, 128), F32),
             pltpu.VMEM((INC, ROWS, 128), F32),
+            pltpu.VMEM((64, 128), jnp.int32),
             pltpu.VMEM((128, 128), F32),
             pltpu.VMEM((128, 128), F32),
             pltpu.VMEM((256, 384), BF),
             pltpu.VMEM((256, 256), BF),
             pltpu.VMEM((4, 128, 128), BF),
-            dma((6 + 2 * NC,)),
+            dma((7 + 3 * NC,)),
             dma((8,)), dma((8,)), dma((NC, 16)), dma((NC, 16)),
             dma((16,)), dma((16,)), dma((8,)), dma((8,)),
-            dma((2,)), dma((2,)), dma((2, NC, 9)), dma((2, NC, 9)),
+            dma((9,)), dma((9,)), dma((2, NC, 9)), dma((2, NC, 9)),
             dma((NC,)), dma((NC,)), dma((NC, 16)), dma((NC, 16)),
             dma((8,)), dma((8,)),
         ],
@@ -415,7 +454,7 @@
             collective_id=0, has_side_effects=True, vmem_limit_bytes=60 * 1024 * 1024
         ),
         name="county_step",
-    )(cont_value, move_cost, mass, live_mask, trans_weight, asset_policy.reshape(64, 128))
+    )(cont_value, move_cost, mass, live_mask, trans_weight, asset_policy)
     return flow_util + v, nm.reshape(ROWS, 1024)
 
 

time: 122 us -> 107 us (0.88)
  Pallas kernels: 116 us -> 102 us
    pallas_call x1, Pallas kernels: 116 us -> 102 us  [shards(): pl.pallas_call(body, out_shape=(jax.ShapeDtypeStruct((ROWS, 1024), F32),...]
where the time goes in v3:
time: 107 us
  Pallas kernels  102 us (95%)
  local copies, waits for them, and re-layouts  2.59 us (2%)
  other arithmetic  2.21 us (2%)
    pallas_call x1, Pallas kernels, shards(): pl.pallas_call(body, out_shape=(jax.ShapeDtypeStruct((ROWS, 1024), F32),...  102 us
    add x1, other arithmetic, shards(): return (flow_util + v, nm.reshape(ROWS, 1024))  2.21 us

profile of v3, /device:TPU:1, one launch (start us, length us, event | category | flops | bytes accessed | tf_op | source)
XLA Modules:
  0.0 107.2 jit_solution(9267420433403825113)
XLA Ops:
  0.6 0.0 copy-start
  0.6 1.6 %copy.9.pol = s32[128,64]{1,0:T(8,128)} copy(s32[128,64]{0,1:T(8,128)} %param.12) | data formatting | bytes 65536 | tf_op args[5]
  2.2 101.7 %county_step.1 = (f32[200,1024]{1,0:T(8,128)}, f32[1600,128]{1,0:T(8,128)}) custom-call(f32[200,1024]{1,0:T(8,128)} %cont_h.1, f32[200,3200]{1,0:T(8,128)} %mc_h.1, f32[200,1024]{1,0:T(8,128)} %mass_h.1, s32[200]{0:T(256)} %live.1, f32[128,128]{1,0:T(8,128)} %tw.1, s32[128,64]{1,0:T(8,128)} %copy.9.pol), custom_call_target="tpu_custom_call" | custom-call | tf_op jit(solution)/shard_map/county_step/pallas_call | solution.py:401
  103.9 0.0 copy-start.1
  103.9 0.0 copy-done
  103.9 2.2 %add.3 = f32[200,1024]{1,0:T(8,128)} add(f32[200,1024]{1,0:T(8,128)S(1)} %copy-done, f32[200,1024]{1,0:T(8,128)} %get-tuple-element.4) | non-fusion elementwise | flops 204800 | bytes 2457600 | tf_op jit(solution)/shard_map/add | solution.py:458
  106.1 0.0 copy-done.1
  106.1 1.0 reshape.7
Async XLA Ops:
  0.6 103.3 %copy-start = (f32[200,1024]{1,0:T(8,128)S(1)}, f32[200,1024]{1,0:T(8,128)}, u32[]{:S(2)}) copy-start(f32[200,1024]{1,0:T(8,128)} %param.8) | copy-start | bytes 2457604
  103.9 2.2 %copy-start.1 = (f32[1600,128]{1,0:T(8,128)S(1)}, f32[1600,128]{1,0:T(8,128)}, u32[]{:S(2)}) copy-start(f32[1600,128]{1,0:T(8,128)} %get-tuple-element.5) | copy-start | bytes 2457604

commit v4 on v3

--- a/solution.py
+++ b/solution.py
@@ -45,7 +45,7 @@
     cont, mc, mass,
     ko, kt, kr, abuf, rbuf, sb, ssend, msd, mrv, mds, mdr, fb, fc, kp, dall, shall, mz, msnd,
     tots, vown, vsend, sfr, csf, cs, cr, xf, ns,
-    gsc, pscr, ptscr, pfwd, pbwd, onehot,
+    psc, gsc, pscr, ptscr, pfwd, pbwd, onehot,
     lsem, s1, r1, s2, r2, sm, rm, sd, rd, sk, rk, sg, rg, sv, rv, s3, r3, s4, r4,
 ):
     li = lax.axis_index("loc")
@@ -113,7 +113,10 @@
 
     pl.semaphore_wait(barrier, PLANE - 1 + 7)
     beside = dev(1 - xh, z, c, ii + 1 - 2 * lax.rem(ii, 2))
-    ksend = [send(ko, kr.at[xh], sk.at[0], rk.at[0], beside)]
+    y = ii // 2
+    part = pl.ds(y * 2, 2)
+    kfirst = send(ko.at[part], kr.at[xh, part], sk.at[0], rk.at[0], beside)
+    ksend = []
 
     a2a = []
     for d in range(1, INC):
@@ -170,9 +173,10 @@
 
     lane64 = lax.broadcasted_iota(jnp.int32, (64, 128), 1)
     lane_low = lane64 < 64
-    gsc[...] = jnp.concatenate(
-        [pol[pl.ds(0, 64, stride=2), :], pol[pl.ds(1, 64, stride=2), :] + 64], axis=1
-    )
+    tall = jnp.concatenate([pol[...].astype(F32), jnp.zeros((64, 128), F32)], axis=0)
+    psc[...] = tall.T
+    odd = pltpu.roll(psc[pl.ds(1, 64, stride=2), :] + 64.0, 64, axis=1)
+    gsc[...] = jnp.where(lane_low, psc[pl.ds(0, 64, stride=2), :], odd).astype(jnp.int32)
     gidx = gsc[...]
     gown = gsc[pl.ds(g * 4, 4), :]
     for t in range(4):
@@ -220,6 +224,12 @@
         ]
         owns[h] = local(ssend.at[h, g], fb.at[h, slot], 5 + h)
 
+    kfirst.wait_recv()
+    for d in (2, 1, 3):
+        ref = kr.at[1 - xh, part]
+        to = dev(xh, z, c, lax.rem(ii + 2 * d, INC))
+        ksend.append(send(ref, ref, sk.at[8 + d], rk.at[8 + d], to))
+
     in3.wait()
     mz[xh] = mass[:, pl.ds(pl.multiple_of(xh * 512, 512), 512)].astype(BF)
     msnd[...] = mass[:, pl.ds(pl.multiple_of((1 - xh) * 512, 512), 512)].astype(BF)
@@ -237,14 +247,6 @@
     for cp in maxes:
         cp.wait_recv()
     cmax = jnp.max(mdr[...], axis=0)
-
-    ownk.wait()
-    for cp in ksend:
-        cp.wait_recv()
-    for x2 in range(2):
-        for b in range(8):
-            dst = (b * 2 + x2) * ROWS
-            kp[1 - xh, :, dst : dst + ROWS] = kr[x2, b]
 
     my_rows = pl.ds(pl.multiple_of(blk * 400, 16), 400)
 
@@ -297,10 +299,21 @@
             dall[h, my_rows, lanes] = jnp.exp(fc[:, lanes] - cmax[k : k + 1, :]).astype(BF)
         gather0(0, dall, h)
 
+    def take_kernel(h):
+        if h > 0:
+            return
+        ownk.wait()
+        for cp in ksend:
+            cp.wait_recv()
+        for x2 in range(2):
+            for b in range(8):
+                dst = (b * 2 + x2) * ROWS
+                kp[1 - xh, :, dst : dst + ROWS] = kr[x2, b]
+        msend.wait_recv()
+
     def st_share(h):
+        take_kernel(h)
         gather3(0, dall, h)
-        if h == 0:
-            msend.wait_recv()
         for x2 in range(2):
             tots[x2] = jnp.dot(kp[x2], dall[h], preferred_element_type=F32)
         sh = []
@@ -366,8 +379,8 @@
             first = k * 4 * MINE + h * PIECE
             xf[first : first + PIECE, :] = cr[h, k].astype(F32)
 
-    @pl.loop(0, 5)
-    def _(i):
+    a2a = []
+    for i in range(5):
         x = jnp.concatenate(
             [xf[pl.ds(i * 5 + t, 64, stride=MINE), :] for t in range(5)], axis=1
         ).astype(BF)
@@ -375,13 +388,15 @@
         o = jnp.dot(pbwd[...], stack, preferred_element_type=F32)
         for t in range(5):
             e = fold(o[:, t * 128 : (t + 1) * 128], lane_low)
-            ns[:, pl.ds(pl.multiple_of(i * 40 + t * 8, 8), 8), :] = e.reshape(8, 8, 128)
-
+            ns[:, i * 40 + t * 8 : i * 40 + t * 8 + 8, :] = e.reshape(8, 8, 128)
+        there = pl.ds(pl.multiple_of(ii * ROWS + i * 40, 8), 40)
+        for d in range(1, INC):
+            peer = lax.rem(ii + d, INC)
+            a2a.append(send(
+                ns.at[peer, pl.ds(i * 40, 40)], nm_out.at[there],
+                s4.at[i, d], r4.at[i, d], (li, peer),
+            ))
     mine = pl.ds(pl.multiple_of(ii * ROWS, 8), ROWS)
-    a2a = []
-    for d in range(1, INC):
-        peer = lax.rem(ii + d, INC)
-        a2a.append(send(ns.at[peer], nm_out.at[mine], s4.at[d], r4.at[d], (li, peer)))
     own4 = local(ns.at[ii], nm_out.at[mine], 5 + 2 * NC)
     own4.wait()
     for cp in a2a:
@@ -437,6 +452,7 @@
             pltpu.VMEM((NC, PLANE, PIECE, 128), BF),
             pltpu.VMEM((MINE * 64, 128), F32),
             pltpu.VMEM((INC, ROWS, 128), F32),
+            pltpu.VMEM((128, 128), F32),
             pltpu.VMEM((64, 128), jnp.int32),
             pltpu.VMEM((128, 128), F32),
             pltpu.VMEM((128, 128), F32),
@@ -446,15 +462,15 @@
             dma((7 + 3 * NC,)),
             dma((8,)), dma((8,)), dma((NC, 16)), dma((NC, 16)),
             dma((16,)), dma((16,)), dma((8,)), dma((8,)),
-            dma((9,)), dma((9,)), dma((2, NC, 9)), dma((2, NC, 9)),
+            dma((12,)), dma((12,)), dma((2, NC, 9)), dma((2, NC, 9)),
             dma((NC,)), dma((NC,)), dma((NC, 16)), dma((NC, 16)),
-            dma((8,)), dma((8,)),
+            dma((5, 8)), dma((5, 8)),
         ],
         compiler_params=pltpu.CompilerParams(
             collective_id=0, has_side_effects=True, vmem_limit_bytes=60 * 1024 * 1024
         ),
         name="county_step",
-    )(cont_value, move_cost, mass, live_mask, trans_weight, asset_policy)
+    )(cont_value, move_cost, mass, live_mask, trans_weight, asset_policy.T)
     return flow_util + v, nm.reshape(ROWS, 1024)
 
 

time: 107 us -> 97.8 us (0.914)
  Pallas kernels: 102 us -> 93.7 us
  local copies, waits for them, and re-layouts: 2.59 us -> 1.02 us
    pallas_call x1, Pallas kernels: 102 us -> 93.7 us  [shards(): pl.pallas_call(body, out_shape=(jax.ShapeDtypeStruct((ROWS, 1024), F32),...]
    unnamed x5 -> x4, local copies, waits for them, and re-layouts: 1.57 us -> 0.01 us
where the time goes in v4:
time: 97.8 us; the launch traced here: 97.7 us
  Pallas kernels  93.7 us (96%)
  other arithmetic  2.23 us (2%)
  local copies, waits for them, and re-layouts  1.02 us (1%)
    pallas_call x1, Pallas kernels, shards(): pl.pallas_call(body, out_shape=(jax.ShapeDtypeStruct((ROWS, 1024), F32),...  93.7 us
    add x1, other arithmetic, shards(): return (flow_util + v, nm.reshape(ROWS, 1024))  2.23 us

profile of v4, /device:TPU:1, one launch (start us, length us, event | category | flops | bytes accessed | tf_op | source)
XLA Modules:
  0.0 97.7 jit_solution(15188468561960944815)
XLA Ops:
  0.6 0.0 copy-start
  0.6 93.7 %county_step.1 = (f32[200,1024]{1,0:T(8,128)}, f32[1600,128]{1,0:T(8,128)}) custom-call(f32[200,1024]{1,0:T(8,128)} %cont_h.1, f32[200,3200]{1,0:T(8,128)} %mc_h.1, f32[200,1024]{1,0:T(8,128)} %mass_h.1, s32[200]{0:T(256)} %live.1, f32[128,128]{1,0:T(8,128)} %tw.1, s32[64,128]{1,0:T(8,128)} %bitcast.1), custom_call_target="tpu_custom_call" | custom-call | tf_op jit(solution)/shard_map/county_step/pallas_call | solution.py:416
  94.4 0.0 copy-start.1
  94.4 0.0 copy-done
  94.4 2.2 %add.3 = f32[200,1024]{1,0:T(8,128)} add(f32[200,1024]{1,0:T(8,128)S(1)} %copy-done, f32[200,1024]{1,0:T(8,128)} %get-tuple-element.4) | non-fusion elementwise | flops 204800 | bytes 2457600 | tf_op jit(solution)/shard_map/add | solution.py:474
  96.6 0.0 copy-done.1
  96.6 1.0 %reshape.7 = f32[200,1024]{1,0:T(8,128)} reshape(f32[1600,128]{1,0:T(8,128)S(1)} %copy-done.1) | data formatting | bytes 1638400 | tf_op jit(solution)/shard_map/reshape | solution.py:474
Async XLA Ops:
  0.6 93.8 %copy-start = (f32[200,1024]{1,0:T(8,128)S(1)}, f32[200,1024]{1,0:T(8,128)}, u32[]{:S(2)}) copy-start(f32[200,1024]{1,0:T(8,128)} %param.8) | copy-start | bytes 2457604
  94.4 2.3 %copy-start.1 = (f32[1600,128]{1,0:T(8,128)S(1)}, f32[1600,128]{1,0:T(8,128)}, u32[]{:S(2)}) copy-start(f32[1600,128]{1,0:T(8,128)} %get-tuple-element.5) | copy-start | bytes 2457604
